TPU v7x, 32 devices: a whole 2x2x4 slice. The times are simulated.
32 devices in a mesh: groups: 2 (over x), seq: 16 (over z, y, core).
Axes of the slice: x: 2, y: 2, z: 4, core: 2. Of those that a mesh axis runs over, the one named last changes fastest.
Arguments:
- tokens: bfloat16 [1024, 512, 512], P(('groups', 'seq')), parts along dimension 0, may hold values from -6 to 6
- cotangent: bfloat16 [1024, 512, 512], P('groups', 'seq'), parts along dimension 0, may hold values from -6 to 6
- w_first: bfloat16 [512, 512], P('seq'), may hold values from -0.25 to 0.25
- w_second: bfloat16 [512, 512], P('seq'), may hold values from -0.25 to 0.25
- mask_first: int32 [4, 4], replicated, may hold values from 0 to 1, as said below
- mask_second: int32 [4, 4], replicated, may hold values from 0 to 1, as said below
- gate_values: bfloat16 [1024, 512], P(('groups', 'seq')), parts along dimension 0, may hold values from -4 to 4
Outputs:
- grad_tokens: bfloat16 [1024, 512, 512], P(('groups', 'seq')), parts along dimension 0
- grad_first: float32 [1024, 512], P(('groups', 'seq')), parts along dimension 0
- grad_second: float32 [1024, 512], P(('groups', 'seq')), parts along dimension 0
There are 2 independent parts, one for each index of `groups`. A program takes and returns all parts, laid end to end along the dimension named above; an argument that names none is the same for every part. Nothing has to cross between parts.
Inputs may be any that keep to these rules, and one draw needn't show every extreme that they name: `mask_first`: the diagonal blocks of each factor are always kept. `mask_second`: the diagonal blocks of each factor are always kept.
All inputs are finite; a program needn't handle non-finite values.
Results may differ from a plain program's by a relative error of at most 0.0054.
Values may be sent and summed in bfloat16 or wider, within the bound.
A program may use at most 320 MiB of HBM per device.

v0:
```python
import math
import jax
import jax.numpy as jnp
from jax import lax
from jax.sharding import PartitionSpec as P

BLK = 128


def expand_rows(mask, row_ids, extent):
    labels = jnp.arange(mask.shape[0], dtype=jnp.int32)
    row_pick = ((row_ids // BLK)[:, None] == labels[None, :]).astype(jnp.float32)
    col_pick = ((jnp.arange(extent, dtype=jnp.int32) // BLK)[:, None] == labels[None, :]).astype(
        jnp.float32
    )
    return jnp.dot(jnp.dot(row_pick, mask.astype(jnp.float32)), col_pick.T)


def per_device(tokens, cotangent, w_first, w_second, mask_first, mask_second, gate_values):
    position = lax.axis_index("seq")
    extent = tokens.shape[1]
    channels = tokens.shape[2]
    shard_rows = w_first.shape[0]
    row_ids = position * shard_rows + jnp.arange(shard_rows, dtype=jnp.int32)
    keep_first = expand_rows(mask_first, row_ids, extent)
    keep_second = expand_rows(mask_second, row_ids, extent)
    local_first = (w_first.astype(jnp.float32) * keep_first).astype(jnp.bfloat16)
    local_second = (w_second.astype(jnp.float32) * keep_second).astype(jnp.bfloat16)
    full = lax.all_gather(jnp.stack([local_first, local_second]), "seq", axis=1, tiled=True)
    full_first, full_second = (full[0], full[1])
    shards = extent // shard_rows
    flat_cot = cotangent.reshape(extent, -1)
    back_flat = lax.dot_general(
        full_second, flat_cot, (((0,), (0,)), ((), ())), preferred_element_type=jnp.float32
    )
    back_col = back_flat.astype(jnp.bfloat16).reshape(cotangent.shape)
    back_rows = lax.all_to_all(back_col, "seq", split_axis=0, concat_axis=1, tiled=True)
    tokens_late, back_col = lax.optimization_barrier((tokens, back_col))
    gate_full = gate_values.astype(jnp.float32)[:, :, None]
    gated = tokens_late.astype(jnp.float32) * gate_full
    hidden = jnp.einsum("ijc,kj->ikc", tokens_late, full_first, preferred_element_type=jnp.float32)
    mixed = (hidden * gated).astype(jnp.bfloat16)
    mixed, back_rows = lax.optimization_barrier((mixed, back_rows))
    columns = lax.all_to_all(mixed, "seq", split_axis=1, concat_axis=0, tiled=True)
    flat_cols = columns.reshape(extent, -1)
    back_float = back_rows.astype(jnp.float32)
    back_hidden = (back_float * gated).astype(jnp.bfloat16)
    direct = gate_full * back_float * hidden
    through = jnp.einsum("ikc,kj->ijc", back_hidden, full_first, preferred_element_type=jnp.float32)
    grad_tokens = (direct + through).astype(jnp.bfloat16)
    summed_first = lax.psum_scatter(
        jnp.einsum("ikc,ijc->kj", back_hidden, tokens_late, preferred_element_type=jnp.float32),
        "seq",
        scatter_dimension=0,
        tiled=True,
    )
    part_second = lax.dot_general(
        flat_cot, flat_cols, (((1,), (1,)), ((), ())), preferred_element_type=jnp.float32
    )
    spread = lax.all_to_all(
        part_second.reshape(shards, shard_rows, extent),
        "seq",
        split_axis=0,
        concat_axis=0,
        tiled=True,
    )
    summed_second = jnp.sum(spread, axis=0)
    factor = 1.0 / math.sqrt(extent * channels)
    grad_first = keep_first * summed_first * factor
    grad_second = keep_second * summed_second * factor
    return (grad_tokens, grad_first, grad_second)


def solution(mesh):
    in_specs = (
        P(("groups", "seq"), None, None),
        P("groups", "seq", None),
        P("seq", None),
        P("seq", None),
        P(),
        P(),
        P(("groups", "seq"), None),
    )
    out_specs = (
        P(("groups", "seq"), None, None),
        P(("groups", "seq"), None),
        P(("groups", "seq"), None),
    )
    return jax.shard_map(
        per_device, mesh=mesh, in_specs=in_specs, out_specs=out_specs, check_vma=False
    )
```

profile of v0, /device:TPU:0, one launch (start us, length us, event | category | flops | bytes accessed | tf_op | source)
XLA Modules:
  0.0 964.3 jit_solution(4726643977585891241)
XLA Ops:
  7.2 0.0 all-gather.2.cloned.1.call-start
  7.2 1.1 fusion.14
  8.3 1.1 fusion.17
  9.4 0.8 fusion.23
  10.2 0.6 pad_maximum_fusion
  10.9 0.0 all-gather.2.cloned.1.call-update
  10.9 18.5 %copy.21 = bf16[64,8,32,512]{3,1,2,0:T(8,128)(2,1)} copy(bf16[64,8,32,512]{3,2,1,0:T(8,128)(2,1)} %bitcast.58) | data formatting | bytes 33554432
  29.3 0.0 copy-done.2
  29.3 22.4 %all-gather.2.cloned.1.call-done = bf16[2,512,512]{2,1,0:T(8,128)(2,1)} async-done(((bf16[2,32,512]{2,1,0:T(8,128)(2,1)}), bf16[2,512,512]{2,1,0:T(8,128)(2,1)}) %all-gather.2.cloned.1.call-update) | async-done | bytes 1048592 | tf_op jit(solution)/shard_map/all_gather | solution.py:29
  51.7 15.8 %convolution_convert_fusion = bf16[512,16384]{1,0:T(8,128)(2,1)} fusion(bf16[512,16384]{1,0:T(8,128)(2,1)} %bitcast.53, bf16[2,512,512]{2,1,0:T(8,128)(2,1)} %all-gather.2.cloned.1.call-done), kind=kOutput, calls=%fused_computation.9 | convolution fusion | flops 8598323200 | bytes 34078720 | tf_op jit(solution)/shard_map/dot_general | solution.py:33
  67.5 16.6 %copy.22 = bf16[64,8,32,512]{3,2,1,0:T(8,128)(2,1)} copy(bf16[64,8,32,512]{3,1,2,0:T(8,128)(2,1)} %bitcast.55) | data formatting | bytes 33554432
  84.0 5.5 all-to-all-start
  89.6 28.2 %fusion.4 = (bf16[32,512,512]{2,1,0:T(8,128)(2,1)}, f32[512,32,512]{2,0,1:T(8,128)}) fusion(bf16[32,512,512]{2,1,0:T(8,128)(2,1)} %param.7, f32[32,512]{1,0:T(8,128)S(1)} %convert_element_type.43, bf16[2,512,512]{2,1,0:T(8,128)(2,1)S(1)} %copy-done.1), kind=kOutput, calls=%fused_computation.7 | convolution fusion | flops 8623489024 | bytes 84475904 | tf_op jit(solution)/shard_map/ijc,kj->ikc/dot_general | solution.py:41
  117.7 268.3 %all-to-all-done = bf16[512,32,512]{2,1,0:T(8,128)(2,1)} async-done(((bf16[512,32,512]{2,1,0:T(8,128)(2,1)}), bf16[512,32,512]{2,1,0:T(8,128)(2,1)}, u32[]{:S(2)}, u32[]{:S(2)}) %all-to-all-start) | async-done | bytes 16777248 | tf_op jit(solution)/shard_map/all_to_all | solution.py:37
  386.0 15.1 %copy.15 = bf16[16,32,32,512]{3,2,0,1:T(8,128)(2,1)} copy(bf16[16,32,32,512]{3,2,1,0:T(8,128)(2,1)} %bitcast.6) | data formatting | bytes 33554432 | tf_op jit(solution)/shard_map/all_to_all | solution.py:37
  401.1 1.8 copy-done
  402.9 26.5 %copy.17 = bf16[32,512,512]{2,0,1:T(8,128)(2,1)} copy(bf16[32,512,512]{2,1,0:T(8,128)(2,1)S(1)} %copy-done) | data formatting | bytes 33554432 | tf_op jit(solution)/shard_map/optimization_barrier | solution.py:43
  429.4 70.2 %all-to-all-start.1 = ((bf16[32,512,512]{2,0,1:T(8,128)(2,1)}), bf16[32,512,512]{2,0,1:T(8,128)(2,1)}, u32[]{:S(2)}, u32[]{:S(2)}) async-start(bf16[32,512,512]{2,0,1:T(8,128)(2,1)} %copy.17), calls=%async_computation.2 | async-start | bytes 33554432 | tf_op jit(solution)/shard_map/all_to_all | solution.py:44
  499.7 0.3 reduce-scatter.2.cloned.1.call-start
  499.9 24.1 %fusion.11 = f32[512,512]{1,0:T(8,128)} fusion(bf16[32,512,512]{2,1,0:T(8,128)(2,1)} %param.7, bf16[32,512,512]{2,1,0:T(8,128)(2,1)} %bitcast.59, f32[32,512]{1,0:T(8,128)S(1)} %convert_element_type.43), kind=kOutput, calls=%fused_computation.12 | convolution fusion | flops 8631877632 | bytes 34668544 | tf_op jit(solution)/shard_map/ikc,ijc->kj/dot_general | solution.py:52
  524.0 0.0 reduce-scatter.2.cloned.1.call-update
  524.1 278.7 %all-to-all-done.1 = bf16[32,512,512]{2,0,1:T(8,128)(2,1)} async-done(((bf16[32,512,512]{2,0,1:T(8,128)(2,1)}), bf16[32,512,512]{2,0,1:T(8,128)(2,1)}, u32[]{:S(2)}, u32[]{:S(2)}) %all-to-all-start.1) | async-done | bytes 16777248 | tf_op jit(solution)/shard_map/all_to_all | solution.py:44
  802.8 15.8 %copy.18 = bf16[32,16,32,512]{3,2,0,1:T(8,128)(2,1)S(1)} copy(bf16[32,16,32,512]{3,0,2,1:T(8,128)(2,1)} %bitcast.12) | data formatting | bytes 33554432 | tf_op jit(solution)/shard_map/all_to_all | solution.py:44
  818.6 12.2 %copy.23 = bf16[64,8,32,512]{3,1,2,0:T(8,128)(2,1)} copy(bf16[64,8,32,512]{3,2,1,0:T(8,128)(2,1)S(1)} %bitcast.57) | data formatting | bytes 33554432
  830.8 18.0 %fusion.36 = f32[512,512]{0,1:T(8,128)} fusion(bf16[512,16384]{1,0:T(8,128)(2,1)} %bitcast.61, bf16[512,16384]{1,0:T(8,128)(2,1)} %bitcast.54), kind=kOutput, calls=%fused_computation.46 | convolution fusion | flops 8589934592 | bytes 34603008 | tf_op jit(solution)/shard_map/dot_general | solution.py:57
  848.9 70.2 %all-to-all-start.2 = ((f32[16,32,512]{2,1,0:T(8,128)}), f32[16,32,512]{2,1,0:T(8,128)S(1)}, u32[]{:S(2)}, u32[]{:S(2)}) async-start(f32[16,32,512]{2,1,0:T(8,128)} %bitcast.15), calls=%async_computation.3 | async-start | bytes 2097152 | tf_op jit(solution)/shard_map/all_to_all | solution.py:60
  919.1 0.0 copy-start.5
  919.1 36.2 %fusion.2 = bf16[32,512,512]{2,1,0:T(8,128)(2,1)} fusion(bf16[32,512,512]{2,1,0:T(8,128)(2,1)} %bitcast.60, f32[512,32,512]{2,0,1:T(8,128)} %get-tuple-element.10, f32[32,512]{1,0:T(8,128)S(1)} %convert_element_type.43, bf16[32,512,512]{2,1,0:T(8,128)(2,1)} %param.7, bf16[2,512,512]{2,1,0:T(8,128)(2,1)S(1)} %copy-done.1), kind=kOutput, calls=%fused_computation.4 | convolution fusion | flops 8673820672 | bytes 101318656 | tf_op jit(solution)/shard_map/ikc,kj->ijc/dot_general | solution.py:49
  955.3 1.5 multiply_multiply_fusion.1
  956.8 0.0 all-to-all-done.2
  956.8 0.1 reduce_sum.9
  956.9 0.6 multiply_multiply_fusion
  (15 shorter events, 0.0 us)
Async XLA Ops:
  7.2 44.5 %all-gather.2.cloned.1.call-start = ((), (), s32[]{:S(2)}) async-start(), calls=%async_computation.4 | async-start | bytes 1114112 | tf_op jit(solution)/shard_map/all_gather | solution.py:29
  8.3 21.0 %copy-start.2 = (f32[32,512]{1,0:T(8,128)}, f32[32,512]{1,0:T(8,128)S(1)}, u32[]{:S(2)}) copy-start(f32[32,512]{1,0:T(8,128)S(1)} %fusion.14) | copy-start | bytes 196612
  9.4 19.9 %copy-start.4 = (f32[32,512]{1,0:T(8,128)}, f32[32,512]{1,0:T(8,128)S(1)}, u32[]{:S(2)}) copy-start(f32[32,512]{1,0:T(8,128)S(1)} %fusion.17) | copy-start | bytes 196612
  84.0 5.5 copy-start.6
  84.0 5.5 copy-start.1
  84.0 302.0 %all-to-all-start = ((bf16[512,32,512]{2,1,0:T(8,128)(2,1)}), bf16[512,32,512]{2,1,0:T(8,128)(2,1)}, u32[]{:S(2)}, u32[]{:S(2)}) async-start(bf16[512,32,512]{2,1,0:T(8,128)(2,1)} %bitcast.56), calls=%async_computation | async-start | bytes 33554432 | tf_op jit(solution)/shard_map/all_to_all | solution.py:37
  386.0 16.9 %copy-start = (bf16[32,512,512]{2,1,0:T(8,128)(2,1)S(1)}, bf16[32,512,512]{2,1,0:T(8,128)(2,1)}, u32[]{:S(2)}) copy-start(bf16[32,512,512]{2,1,0:T(8,128)(2,1)} %get-tuple-element.8) | copy-start | bytes 50331652
  429.4 373.4 %all-to-all-start.1 = ((bf16[32,512,512]{2,0,1:T(8,128)(2,1)}), bf16[32,512,512]{2,0,1:T(8,128)(2,1)}, u32[]{:S(2)}, u32[]{:S(2)}) async-start(bf16[32,512,512]{2,0,1:T(8,128)(2,1)} %copy.17), calls=%async_computation.2 | async-start | bytes 33554432 | tf_op jit(solution)/shard_map/all_to_all | solution.py:44
  499.7 455.6 %reduce-scatter.2.cloned.1.call-start = ((), (), s32[]{:S(2)}) async-start(), calls=%async_computation.5 | async-start | bytes 1114112 | tf_op jit(solution)/shard_map/reduce_scatter | solution.py:51
  848.9 107.9 %all-to-all-start.2 = ((f32[16,32,512]{2,1,0:T(8,128)}), f32[16,32,512]{2,1,0:T(8,128)S(1)}, u32[]{:S(2)}, u32[]{:S(2)}) async-start(f32[16,32,512]{2,1,0:T(8,128)} %bitcast.15), calls=%async_computation.3 | async-start | bytes 2097152 | tf_op jit(solution)/shard_map/all_to_all | solution.py:60
  919.1 36.2 %copy-start.5 = (f32[32,512]{1,0:T(8,128)S(1)}, f32[32,512]{1,0:T(8,128)}, u32[]{:S(2)}) copy-start(f32[32,512]{1,0:T(8,128)} %copy-done.4) | copy-start | bytes 196612
  919.1 37.7 %copy-start.3 = (f32[32,512]{1,0:T(8,128)S(1)}, f32[32,512]{1,0:T(8,128)}, u32[]{:S(2)}) copy-start(f32[32,512]{1,0:T(8,128)} %copy-done.2) | copy-start | bytes 196612
Sparse Core Ops, SparseCore 0:
  11.0 40.6 all-gather.1
  524.2 257.9 reduce-scatter.1
where the time goes:
time: 965 us; the launch traced here: 964 us
  waiting for transfers between devices  569 us (59%)
  starting transfers between devices  146 us (15%)
  matrix products  124 us (13%)
  local copies, waits for them, and re-layouts  106 us (11%)
  between operations  14.2 us (1%)
    all_to_all x1, waiting for transfers between devices, per_device(): lax.all_to_all(mixed, 'seq', split_axis=1, concat_axis=0, tiled=True)  279 us
    all_to_all x1, waiting for transfers between devices, per_device(): lax.all_to_all(back_col, 'seq', split_axis=0, concat_axis=1, tiled=True)  268 us
    all_to_all x1, starting transfers between devices, per_device(): lax.all_to_all(part_second.reshape(shards, shard_rows, extent), 'seq', sp...  70.2 us
    all_to_all x1, starting transfers between devices, per_device(): lax.all_to_all(mixed, 'seq', split_axis=1, concat_axis=0, tiled=True)  70.2 us
    unnamed x17, local copies, waits for them, and re-layouts  49 us
    dot_general x1, matrix products, per_device(): jnp.einsum('ikc,kj->ijc', back_hidden, full_first, preferred_element_type...  36.2 us
    dot_general x1, matrix products, per_device(): jnp.einsum('ijc,kj->ikc', tokens_late, full_first, preferred_element_type...  28.2 us
    optimization_barrier x1, local copies, waits for them, and re-layouts, per_device(): mixed, back_rows = lax.optimization_barrier((mixed, back_rows))  26.5 us
  transfers between devices with their start and end apart: 5, of which 3 were waited for; matrix products, arithmetic and copies ran while one was open for 16% of the time, Pallas kernels for 0%

commit v1 on v0

--- a/solution.py
+++ b/solution.py
@@ -5,6 +5,18 @@
 from jax.sharding import PartitionSpec as P
 
 BLK = 128
+
+
+def doubled_up(x, axis, dim):
+    ways, here = (lax.axis_size(axis), lax.axis_index(axis))
+    grown, reach = (x, 1)
+    while reach < ways:
+        theirs = lax.ppermute(grown, axis, [(d, d ^ reach) for d in range(ways)])
+        mine_first = jnp.concatenate([grown, theirs], axis=dim)
+        theirs_first = jnp.concatenate([theirs, grown], axis=dim)
+        grown = jnp.where(here & reach == 0, mine_first, theirs_first)
+        reach = 2 * reach
+    return grown
 
 
 def expand_rows(mask, row_ids, extent):
@@ -26,7 +38,7 @@
     keep_second = expand_rows(mask_second, row_ids, extent)
     local_first = (w_first.astype(jnp.float32) * keep_first).astype(jnp.bfloat16)
     local_second = (w_second.astype(jnp.float32) * keep_second).astype(jnp.bfloat16)
-    full = lax.all_gather(jnp.stack([local_first, local_second]), "seq", axis=1, tiled=True)
+    full = doubled_up(jnp.stack([local_first, local_second]), "seq", 1)
     full_first, full_second = (full[0], full[1])
     shards = extent // shard_rows
     flat_cot = cotangent.reshape(extent, -1)

time: 965 us -> 968 us (level)
    all_gather x1 -> x0, waiting for transfers between devices: 22.4 us -> none  [per_device(): lax.all_gather(jnp.stack([local_first, local_second]), 'seq', axis=1, til...]
    ppermute x0 -> x4, waiting for transfers between devices: none -> 14.6 us  [doubled_up(): theirs = lax.ppermute(grown, axis, [(d, d ^ reach) for d in range(ways)])]
    unnamed x17 -> x15, local copies, waits for them, and re-layouts: 49 us -> 49 us
  transfers between devices with their start and end apart: 5 -> 8, of which waited for: 3 -> 6; matrix products, arithmetic and copies ran while one was open for 16% -> 16% of each run, Pallas kernels for 0% -> 0%
where the time goes in v1:
time: 968 us; the launch traced here: 967 us
  waiting for transfers between devices  562 us (58%)
  starting transfers between devices  154 us (16%)
  matrix products  127 us (13%)
  local copies, waits for them, and re-layouts  106 us (11%)
  between operations  14.2 us (1%)
    all_to_all x1, waiting for transfers between devices, per_device(): lax.all_to_all(mixed, 'seq', split_axis=1, concat_axis=0, tiled=True)  279 us
    all_to_all x1, waiting for transfers between devices, per_device(): lax.all_to_all(back_col, 'seq', split_axis=0, concat_axis=1, tiled=True)  269 us
    all_to_all x1, starting transfers between devices, per_device(): lax.all_to_all(mixed, 'seq', split_axis=1, concat_axis=0, tiled=True)  70.2 us
    all_to_all x1, starting transfers between devices, per_device(): lax.all_to_all(part_second.reshape(shards, shard_rows, extent), 'seq', sp...  70.2 us
    unnamed x15, local copies, waits for them, and re-layouts  49 us
    dot_general x1, matrix products, per_device(): jnp.einsum('ikc,kj->ijc', back_hidden, full_first, preferred_element_type...  36.2 us
    dot_general x1, matrix products, per_device(): jnp.einsum('ijc,kj->ikc', tokens_late, full_first, preferred_element_type...  28.2 us
    optimization_barrier x1, local copies, waits for them, and re-layouts, per_device(): mixed, back_rows = lax.optimization_barrier((mixed, back_rows))  26.5 us
  transfers between devices with their start and end apart: 8, of which 6 were waited for; matrix products, arithmetic and copies ran while one was open for 16% of the time, Pallas kernels for 0%

profile of v1, /device:TPU:0, one launch (start us, length us, event | category | flops | bytes accessed | tf_op | source)
XLA Modules:
  0.0 967.2 jit_solution(1456014706451392458)
XLA Ops:
  7.2 1.1 fusion.14
  8.3 1.1 fusion.17
  9.4 0.8 fusion.23
  10.2 0.5 collective-permute-start
  10.7 0.9 collective-permute-done
  11.6 2.9 collective-permute-start.1
  14.6 3.8 collective-permute-done.1
  18.4 1.9 collective-permute-start.2
  20.3 6.1 collective-permute-done.2
  26.6 2.6 collective-permute-start.3
  29.1 18.4 %copy.21 = bf16[64,8,32,512]{3,1,2,0:T(8,128)(2,1)} copy(bf16[64,8,32,512]{3,2,1,0:T(8,128)(2,1)} %bitcast.58) | data formatting | bytes 33554432
  47.6 3.8 collective-permute-done.3
  51.4 0.4 maximum_select_fusion
  51.8 18.2 %convolution_convert_fusion = bf16[512,16384]{1,0:T(8,128)(2,1)} fusion(bf16[512,16384]{1,0:T(8,128)(2,1)} %bitcast.53, bf16[2,512,512]{2,1,0:T(8,128)(2,1)S(1)} %maximum_select_fusion), kind=kOutput, calls=%fused_computation.9 | convolution fusion | flops 8598323200 | bytes 34078720 | tf_op jit(solution)/shard_map/dot_general | solution.py:45
  70.0 16.6 %copy.22 = bf16[64,8,32,512]{3,2,1,0:T(8,128)(2,1)} copy(bf16[64,8,32,512]{3,1,2,0:T(8,128)(2,1)} %bitcast.55) | data formatting | bytes 33554432
  86.5 5.6 all-to-all-start
  92.2 28.2 %fusion.4 = (bf16[32,512,512]{2,1,0:T(8,128)(2,1)}, f32[512,32,512]{2,0,1:T(8,128)}) fusion(bf16[32,512,512]{2,1,0:T(8,128)(2,1)} %param.7, f32[32,512]{1,0:T(8,128)S(1)} %convert_element_type.43, bf16[2,512,512]{2,1,0:T(8,128)(2,1)S(1)} %maximum_select_fusion), kind=kOutput, calls=%fused_computation.7 | convolution fusion | flops 8623489024 | bytes 84475904 | tf_op jit(solution)/shard_map/ijc,kj->ikc/dot_general | solution.py:53
  120.3 268.5 %all-to-all-done = bf16[512,32,512]{2,1,0:T(8,128)(2,1)} async-done(((bf16[512,32,512]{2,1,0:T(8,128)(2,1)}), bf16[512,32,512]{2,1,0:T(8,128)(2,1)}, u32[]{:S(2)}, u32[]{:S(2)}) %all-to-all-start) | async-done | bytes 16777248 | tf_op jit(solution)/shard_map/all_to_all | solution.py:49
  388.9 15.1 %copy.15 = bf16[16,32,32,512]{3,2,0,1:T(8,128)(2,1)} copy(bf16[16,32,32,512]{3,2,1,0:T(8,128)(2,1)} %bitcast.6) | data formatting | bytes 33554432 | tf_op jit(solution)/shard_map/all_to_all | solution.py:49
  404.0 1.8 copy-done
  405.8 26.5 %copy.17 = bf16[32,512,512]{2,0,1:T(8,128)(2,1)} copy(bf16[32,512,512]{2,1,0:T(8,128)(2,1)S(1)} %copy-done) | data formatting | bytes 33554432 | tf_op jit(solution)/shard_map/optimization_barrier | solution.py:55
  432.3 70.2 %all-to-all-start.1 = ((bf16[32,512,512]{2,0,1:T(8,128)(2,1)}), bf16[32,512,512]{2,0,1:T(8,128)(2,1)}, u32[]{:S(2)}, u32[]{:S(2)}) async-start(bf16[32,512,512]{2,0,1:T(8,128)(2,1)} %copy.17), calls=%async_computation.2 | async-start | bytes 33554432 | tf_op jit(solution)/shard_map/all_to_all | solution.py:56
  502.5 0.3 reduce-scatter.2.cloned.1.call-start
  502.8 24.1 %fusion.11 = f32[512,512]{1,0:T(8,128)} fusion(bf16[32,512,512]{2,1,0:T(8,128)(2,1)} %param.7, bf16[32,512,512]{2,1,0:T(8,128)(2,1)} %bitcast.59, f32[32,512]{1,0:T(8,128)S(1)} %convert_element_type.43), kind=kOutput, calls=%fused_computation.12 | convolution fusion | flops 8631877632 | bytes 34668544 | tf_op jit(solution)/shard_map/ikc,ijc->kj/dot_general | solution.py:64
  526.9 278.7 %all-to-all-done.1 = bf16[32,512,512]{2,0,1:T(8,128)(2,1)} async-done(((bf16[32,512,512]{2,0,1:T(8,128)(2,1)}), bf16[32,512,512]{2,0,1:T(8,128)(2,1)}, u32[]{:S(2)}, u32[]{:S(2)}) %all-to-all-start.1) | async-done | bytes 16777248 | tf_op jit(solution)/shard_map/all_to_all | solution.py:56
  805.7 15.8 %copy.18 = bf16[32,16,32,512]{3,2,0,1:T(8,128)(2,1)S(1)} copy(bf16[32,16,32,512]{3,0,2,1:T(8,128)(2,1)} %bitcast.12) | data formatting | bytes 33554432 | tf_op jit(solution)/shard_map/all_to_all | solution.py:56
  821.5 12.2 %copy.23 = bf16[64,8,32,512]{3,1,2,0:T(8,128)(2,1)} copy(bf16[64,8,32,512]{3,2,1,0:T(8,128)(2,1)S(1)} %bitcast.57) | data formatting | bytes 33554432
  833.7 18.0 %fusion.36 = f32[512,512]{0,1:T(8,128)} fusion(bf16[512,16384]{1,0:T(8,128)(2,1)} %bitcast.61, bf16[512,16384]{1,0:T(8,128)(2,1)} %bitcast.54), kind=kOutput, calls=%fused_computation.50 | convolution fusion | flops 8589934592 | bytes 34603008 | tf_op jit(solution)/shard_map/dot_general | solution.py:69
  851.7 70.2 %all-to-all-start.2 = ((f32[16,32,512]{2,1,0:T(8,128)}), f32[16,32,512]{2,1,0:T(8,128)S(1)}, u32[]{:S(2)}, u32[]{:S(2)}) async-start(f32[16,32,512]{2,1,0:T(8,128)} %bitcast.15), calls=%async_computation.3 | async-start | bytes 2097152 | tf_op jit(solution)/shard_map/all_to_all | solution.py:72
  922.0 36.2 %fusion.2 = bf16[32,512,512]{2,1,0:T(8,128)(2,1)} fusion(bf16[32,512,512]{2,1,0:T(8,128)(2,1)} %bitcast.60, f32[512,32,512]{2,0,1:T(8,128)} %get-tuple-element.10, f32[32,512]{1,0:T(8,128)S(1)} %convert_element_type.43, bf16[32,512,512]{2,1,0:T(8,128)(2,1)} %param.7, bf16[2,512,512]{2,1,0:T(8,128)(2,1)S(1)} %maximum_select_fusion), kind=kOutput, calls=%fused_computation.4 | convolution fusion | flops 8673820672 | bytes 101318656 | tf_op jit(solution)/shard_map/ikc,kj->ijc/dot_general | solution.py:61
  958.2 1.5 multiply_multiply_fusion.1
  959.7 0.6 multiply_multiply_fusion
  (22 shorter events, 0.4 us)
Async XLA Ops:
  8.3 6.3 copy-start.1
  9.3 5.2 copy-start.3
  10.2 1.4 collective-permute-start
  11.6 6.8 collective-permute-start.1
  18.4 7.9 collective-permute-start.2
  26.6 24.8 %collective-permute-start.3 = (bf16[2,256,512]{2,1,0:T(8,128)(2,1)S(1)}, bf16[2,256,512]{2,1,0:T(8,128)(2,1)S(1)}, u32[]{:S(2)}, u32[]{:S(2)}) collective-permute-start(bf16[2,256,512]{2,1,0:T(8,128)(2,1)S(1)} %maximum_select_fusion.1), channel_id=1, source_target_pairs={{0,8},{1,9},{2,10},{3,11},{4,12},{5,13},{6,14},{7,15},{8,0},{9,1},... | collective-permute-start | bytes 1572872 | tf_op jit(solution)/shard_map/ppermute | solution.py:14
  86.5 5.6 copy-start.5
  86.5 302.3 %all-to-all-start = ((bf16[512,32,512]{2,1,0:T(8,128)(2,1)}), bf16[512,32,512]{2,1,0:T(8,128)(2,1)}, u32[]{:S(2)}, u32[]{:S(2)}) async-start(bf16[512,32,512]{2,1,0:T(8,128)(2,1)} %bitcast.56), calls=%async_computation | async-start | bytes 33554432 | tf_op jit(solution)/shard_map/all_to_all | solution.py:49
  388.9 16.9 %copy-start = (bf16[32,512,512]{2,1,0:T(8,128)(2,1)S(1)}, bf16[32,512,512]{2,1,0:T(8,128)(2,1)}, u32[]{:S(2)}) copy-start(bf16[32,512,512]{2,1,0:T(8,128)(2,1)} %get-tuple-element.8) | copy-start | bytes 50331652
  432.3 373.4 %all-to-all-start.1 = ((bf16[32,512,512]{2,0,1:T(8,128)(2,1)}), bf16[32,512,512]{2,0,1:T(8,128)(2,1)}, u32[]{:S(2)}, u32[]{:S(2)}) async-start(bf16[32,512,512]{2,0,1:T(8,128)(2,1)} %copy.17), calls=%async_computation.2 | async-start | bytes 33554432 | tf_op jit(solution)/shard_map/all_to_all | solution.py:56
  502.5 455.6 %reduce-scatter.2.cloned.1.call-start = ((), (), s32[]{:S(2)}) async-start(), calls=%async_computation.4 | async-start | bytes 1114112 | tf_op jit(solution)/shard_map/reduce_scatter | solution.py:63
  851.7 107.9 %all-to-all-start.2 = ((f32[16,32,512]{2,1,0:T(8,128)}), f32[16,32,512]{2,1,0:T(8,128)S(1)}, u32[]{:S(2)}, u32[]{:S(2)}) async-start(f32[16,32,512]{2,1,0:T(8,128)} %bitcast.15), calls=%async_computation.3 | async-start | bytes 2097152 | tf_op jit(solution)/shard_map/all_to_all | solution.py:72
  922.0 36.2 %copy-start.4 = (f32[32,512]{1,0:T(8,128)S(1)}, f32[32,512]{1,0:T(8,128)}, u32[]{:S(2)}) copy-start(f32[32,512]{1,0:T(8,128)} %copy-done.3) | copy-start | bytes 196612
  922.0 37.7 %copy-start.2 = (f32[32,512]{1,0:T(8,128)S(1)}, f32[32,512]{1,0:T(8,128)}, u32[]{:S(2)}) copy-start(f32[32,512]{1,0:T(8,128)} %copy-done.1) | copy-start | bytes 196612
Sparse Core Ops, SparseCore 0:
  527.1 257.9 reduce-scatter.1
